TPU v7x, 512 devices: a whole 4x8x8 slice. The times are simulated.
512 devices in a mesh: ctx: 16 (over x, z_hi), row: 8 (over y), batch: 4 (over z_lo, core).
Axes of the slice: x: 4, y: 8, z: 8 (z_hi: 4, z_lo: 2; z = z_hi * 2 + z_lo), core: 2. Of those that a mesh axis runs over, the one named last changes fastest.
Arguments:
- queries: bfloat16 [12288, 5120], P(('batch', 'ctx'), 'row'), parts along dimension 0
- keys: bfloat16 [12288, 5120], P(('batch', 'ctx'), 'row'), parts along dimension 0
- values: bfloat16 [12288, 5120], P(('batch', 'ctx'), 'row'), parts along dimension 0, may hold values from -6 to 6
- gain_q: float32 [5120], P('row'), may hold values from 1.2 to 2.4
- gain_k: float32 [5120], P('row'), may hold values from 1.2 to 2.4
- clip_ids: int32 [12288], P(('batch', 'ctx')), parts along dimension 0, may hold values from 0 to 3, never falling along the last dimension, each value on 1 to 1920 neighbouring positions
- clip_grid: int32 [16, 2], P('batch'), parts along dimension 0, may hold values from 8 to 40
Outputs:
- attended: bfloat16 [12288, 5120], P(('batch', 'ctx'), 'row'), parts along dimension 0
There are 4 independent parts, one for each index of `batch`. A program takes and returns all parts, laid end to end along the dimension named above; an argument that names none is the same for every part. Nothing has to cross between parts.
Inputs may be any that keep to these rules, and one draw needn't show every extreme that they name: `clip_ids`: never falls along the tokens; each of the 4 clips has 1 to 1920 tokens, and one has exactly 1920.
All inputs are finite; a program needn't handle non-finite values.
Results may differ from a plain program's by a relative error of at most 0.012.
The roundings to bfloat16 on the way count: a program that leaves them out, or rounds other values in their place, can miss the bound.
Values may be sent and summed in bfloat16 or wider, within the bound.
A program may use at most 64 MiB of HBM per device.

v0:
```python
import math

import jax
import jax.numpy as jnp
from jax import lax
from jax.sharding import PartitionSpec as P

HD = 128
D = 5120
CLIPS = 4


EPSILON = 1e-06
NEGATIVE = -1e30
ROTARY_BASE = 10000.0
block_limit = 1024


def lookup(lookup_table, positions):
    labels = jnp.arange(lookup_table.shape[0], dtype=jnp.int32)
    return jnp.sum(
        jnp.where(positions[:, None] == labels[None, :], lookup_table[None, :], 0), axis=1
    )


def spin(matrix, offsets, clip_of, clip_grid, head_size):
    row_count = matrix.shape[0]
    sixth_part = head_size // 6
    first_dims = head_size - 4 * sixth_part
    first_freqs = 1.0 / ROTARY_BASE ** (
        jnp.arange(0, first_dims, 2, dtype=jnp.float32) / first_dims
    )
    other_freqs = 1.0 / ROTARY_BASE ** (
        jnp.arange(0, 2 * sixth_part, 2, dtype=jnp.float32) / (2 * sixth_part)
    )
    heights = lookup(clip_grid[:, 0], clip_of)
    widths = lookup(clip_grid[:, 1], clip_of)
    frame_pos = offsets // (heights * widths)
    line_pos = offsets // widths % heights
    column_pos = offsets % widths
    angles = jnp.concatenate(
        [
            frame_pos.astype(jnp.float32)[:, None] * first_freqs[None, :],
            line_pos.astype(jnp.float32)[:, None] * other_freqs[None, :],
            column_pos.astype(jnp.float32)[:, None] * other_freqs[None, :],
        ],
        axis=1,
    )
    cosine = jnp.repeat(jnp.cos(angles), 2, axis=1)
    sine_table = jnp.repeat(jnp.sin(angles), 2, axis=1)
    feature = jnp.arange(head_size, dtype=jnp.int32)
    is_even = (feature % 2 == 0)[None, None, :]
    head_view = matrix.reshape(row_count, -1, head_size)
    partner = jnp.where(is_even, -jnp.roll(head_view, -1, axis=2), jnp.roll(head_view, 1, axis=2))
    turned = head_view * cosine[:, None, :] + partner * sine_table[:, None, :]
    return turned.reshape(row_count, -1)


def on_device(queries, keys, values, gain_q, gain_k, clip_ids, clip_grid):
    rows_here, width_here = queries.shape
    heads_here = width_here // HD
    score_scale = 1.0 / math.sqrt(HD)
    query_wide = queries.astype(jnp.float32)
    key_wide = keys.astype(jnp.float32)
    squares = lax.psum(
        (jnp.sum(query_wide * query_wide, axis=1), jnp.sum(key_wide * key_wide, axis=1)), "row"
    )
    query_scale = lax.rsqrt(squares[0] / D + EPSILON)
    key_scale = lax.rsqrt(squares[1] / D + EPSILON)
    labels = jnp.arange(CLIPS, dtype=jnp.int32)
    local_counts = jnp.sum((clip_ids[:, None] == labels[None, :]).astype(jnp.int32), axis=0)
    totals = lax.psum(local_counts, "ctx")
    starts = jnp.cumsum(totals) - totals
    first_row = lax.axis_index("ctx") * rows_here
    offsets = first_row + jnp.arange(rows_here, dtype=jnp.int32) - lookup(starts, clip_ids)
    query_rot = spin(
        query_wide * query_scale[:, None] * gain_q[None, :], offsets, clip_ids, clip_grid, HD
    ).astype(jnp.bfloat16)
    query_heads = query_rot.reshape(rows_here, heads_here, HD)
    key_send = spin(
        key_wide * key_scale[:, None] * gain_k[None, :], offsets, clip_ids, clip_grid, HD
    ).astype(jnp.bfloat16)
    initial = (
        jnp.full((heads_here, rows_here), NEGATIVE, jnp.float32),
        jnp.zeros((heads_here, rows_here), jnp.float32),
        jnp.zeros((rows_here, heads_here, HD), jnp.float32),
    )
    running = initial
    piece_start = jnp.int32(0)
    key_piece = lax.all_gather(key_send, "ctx", axis=0, tiled=True)
    value_piece = lax.all_gather(values, "ctx", axis=0, tiled=True)
    row_count = key_piece.shape[0]
    block_rows = min(row_count, block_limit)
    for block_first in range(0, row_count, block_rows):
        block_size = min(block_rows, row_count - block_first)
        fold_key_rows = key_piece[block_first : block_first + block_size]
        fold_value_rows = value_piece[block_first : block_first + block_size]
        key_index = piece_start + block_first + jnp.arange(fold_key_rows.shape[0], dtype=jnp.int32)
        key_key_clips = (
            jnp.sum((starts[None, :] <= key_index[:, None]).astype(jnp.int32), axis=1) - 1
        )
        peak_old, total_old, summed_old = running
        key_view = fold_key_rows.reshape(fold_key_rows.shape[0], heads_here, HD)
        value_view = fold_value_rows.reshape(fold_value_rows.shape[0], heads_here, HD)
        scores = (
            jnp.einsum("qhd,khd->hqk", query_heads, key_view, preferred_element_type=jnp.float32)
            * score_scale
        )
        same = clip_ids[:, None] == key_key_clips[None, :]
        masked = jnp.where(same[None, :, :], scores, NEGATIVE)
        peak_new = jnp.maximum(peak_old, jnp.max(masked, axis=2))
        weights = jnp.where(same[None, :, :], jnp.exp(masked - peak_new[:, :, None]), 0.0)
        factor = jnp.exp(peak_old - peak_new)
        total_new = total_old * factor + jnp.sum(weights, axis=2)
        summed = summed_old * jnp.transpose(factor)[:, :, None] + jnp.einsum(
            "hqk,khd->qhd",
            weights.astype(jnp.bfloat16),
            value_view,
            preferred_element_type=jnp.float32,
        )
        running = (peak_new, total_new, summed)
    attended = running[2] / jnp.transpose(running[1])[:, :, None]
    return attended.reshape(rows_here, width_here).astype(jnp.bfloat16)


def solution(mesh):
    in_specs = (
        P(("batch", "ctx"), "row"),
        P(("batch", "ctx"), "row"),
        P(("batch", "ctx"), "row"),
        P("row"),
        P("row"),
        P(("batch", "ctx")),
        P("batch", None),
    )
    out_specs = P(("batch", "ctx"), "row")
    return jax.shard_map(
        on_device, mesh=mesh, in_specs=in_specs, out_specs=out_specs, check_vma=False
    )
```

profile of v0, /device:TPU:1, one launch (start us, length us, event | category | flops | bytes accessed | tf_op | source)
XLA Modules:
  0.0 213.5 jit_solution(10910715953771418640)
XLA Ops:
  6.5 0.7 all-gather.5.cloned.1.call-update
  7.3 0.8 convert_reduce_fusion.3
  8.1 20.5 %psum.21 = s32[4]{0:T(128)S(1)} all-reduce(s32[4]{0:T(128)S(1)} %convert_reduce_fusion.3), channel_id=1, replica_groups=mesh['ctx'=16,'row'=8,'batch'=4] {'ctx'}, use_global_device_ids=true, to_apply=%region_1.0 | all-reduce | flops 4 | bytes 32 | tf_op jit(solution)/shard_map/psum | solution.py:72
  28.8 0.8 slice_bitcast_fusion
  29.6 0.8 select_reduce_fusion.1
  31.3 1.1 copy.45
  32.5 1.1 copy.46
  33.8 15.1 %all-reduce = (f32[192]{0:T(256)S(1)}, f32[192]{0:T(256)S(1)}) all-reduce(f32[192]{0:T(256)S(1)} %fusion.48, f32[192]{0:T(256)S(1)} %fusion.50), channel_id=1, replica_groups=mesh['ctx'=16,'row'=8,'batch'=4] {'row'}, use_global_device_ids=true, to_apply=%region_5.0 | all-reduce | flops 384 | bytes 3072 | tf_op jit(solution)/shard_map/psum | solution.py:65
  49.0 0.8 fusion.49
  50.7 0.4 fusion.55
  51.2 0.9 copy.47
  52.2 0.4 broadcast_compare_fusion
  52.6 44.7 %all-gather.5.cloned.1.call-done = bf16[3072,640]{1,0:T(8,128)(2,1)} async-done(((bf16[192,640]{1,0:T(8,128)(2,1)}), bf16[3072,640]{1,0:T(8,128)(2,1)}) %all-gather.5.cloned.1.call-update) | async-done | bytes 3932176 | tf_op jit(solution)/shard_map/all_gather | solution.py:91
  97.3 4.0 %fusion.81 = (bf16[1024,640]{1,0:T(8,128)(2,1)S(1)}, bf16[1024,640]{1,0:T(8,128)(2,1)}, bf16[1024,640]{1,0:T(8,128)(2,1)}) fusion(bf16[3072,640]{1,0:T(8,128)(2,1)} %all-gather.5.cloned.1.call-done), kind=kLoop, calls=%fused_computation.121 | loop fusion | bytes 7864320 | tf_op jit(solution)/shard_map/slice | solution.py:97
  101.3 1.5 copy.79
  102.8 76.7 %all-gather.3.cloned.1.call-done = bf16[3072,640]{1,0:T(8,128)(2,1)} async-done(((bf16[192,640]{1,0:T(8,128)(2,1)}), bf16[3072,640]{1,0:T(8,128)(2,1)}) %all-gather.3.cloned.1.call-update) | async-done | bytes 3932176 | tf_op jit(solution)/shard_map/all_gather | solution.py:90
  179.5 3.9 %fusion.82 = (bf16[1024,640]{1,0:T(8,128)(2,1)S(1)}, bf16[1024,640]{1,0:T(8,128)(2,1)}, bf16[1024,640]{1,0:T(8,128)(2,1)}) fusion(bf16[3072,640]{1,0:T(8,128)(2,1)} %all-gather.3.cloned.1.call-done), kind=kLoop, calls=%fused_computation.122 | loop fusion | bytes 7864320 | tf_op jit(solution)/shard_map/slice | solution.py:96
  183.4 0.6 copy.78
  184.1 1.6 copy.76
  185.7 2.5 %copy.74 = bf16[1024,640]{0,1:T(8,128)(2,1)} copy(bf16[1024,640]{1,0:T(8,128)(2,1)} %get-tuple-element.22) | data formatting | bytes 2621440
  188.2 2.5 %copy.77 = bf16[1024,640]{0,1:T(8,128)(2,1)} copy(bf16[1024,640]{1,0:T(8,128)(2,1)} %get-tuple-element.18) | data formatting | bytes 2621440
  190.7 2.5 %copy.75 = bf16[1024,640]{0,1:T(8,128)(2,1)} copy(bf16[1024,640]{1,0:T(8,128)(2,1)} %get-tuple-element.19) | data formatting | bytes 2621440
  193.2 2.4 %fusion = (f32[5,192]{1,0:T(8,128)S(1)}, f32[5,192,1024]{2,1,0:T(8,128)S(1)}) fusion(pred[192,1024]{1,0:T(8,128)(4,1)S(1)} %get-tuple-element.43, bf16[192,5,128]{0,2,1:T(8,128)(2,1)S(1)} %bitcast.131, bf16[1024,5,128]{0,2,1:T(8,128)(2,1)} %bitcast.136), kind=kOutput, calls=%fused_computation.6 | convolution fusion | flops 254606400 | bytes 5689088 | tf_op jit(solution)/shard_map/qhd,khd->hqk/dot_general | solution.py:106
  195.6 1.1 fusion.1
  196.6 1.1 fusion.2
  197.7 1.3 fusion.7
  199.0 1.3 fusion.5
  200.3 1.3 fusion.3
  201.6 1.3 fusion.39
  202.9 1.3 fusion.33
  204.3 1.3 fusion.45
  205.8 0.9 copy.64
  (49 shorter events, 2.6 us)
Async XLA Ops:
  6.5 90.7 %all-gather.5.cloned.1.call-start = ((), (), s32[]{:S(2)}) async-start(), calls=%async_computation.1 | async-start | bytes 4177920 | tf_op jit(solution)/shard_map/all_gather | solution.py:91
  7.3 172.2 %all-gather.3.cloned.1.call-start = ((), (), s32[]{:S(2)}) async-start(), calls=%async_computation | async-start | bytes 4177920 | tf_op jit(solution)/shard_map/all_gather | solution.py:90
  31.3 18.8 %copy-start.3 = (f32[640]{0:T(1024)S(1)}, f32[640]{0:T(1024)}, u32[]{:S(2)}) copy-start(f32[640]{0:T(1024)} %param.11) | copy-start | bytes 7684
  50.0 0.7 copy-start.4
  50.4 1.8 copy-start.5
  199.0 2.6 %copy-start.2 = (bf16[1024,640]{0,1:T(8,128)(2,1)S(1)}, bf16[1024,640]{0,1:T(8,128)(2,1)}, u32[]{:S(2)}) copy-start(bf16[1024,640]{0,1:T(8,128)(2,1)} %copy.75) | copy-start | bytes 3932164
  201.6 1.3 copy-start.1
  202.9 1.3 copy-start
Sparse Core Ops, SparseCore 0:
  10.4 86.8 all-gather.4
  100.3 79.1 all-gather.2
where the time goes:
time: 214 us
  waiting for transfers between devices  122 us (57%)
  blocking collectives  35.7 us (17%)
  local copies, waits for them, and re-layouts  24.8 us (12%)
  between operations  13.8 us (6%)
  other arithmetic  8.73 us (4%)
  matrix products  8.44 us (4%)
    all_gather x1, waiting for transfers between devices, on_device(): key_piece = lax.all_gather(key_send, 'ctx', axis=0, tiled=True)  76.7 us
    all_gather x1, waiting for transfers between devices, on_device(): value_piece = lax.all_gather(values, 'ctx', axis=0, tiled=True)  44.7 us
    psum x1, blocking collectives, on_device(): totals = lax.psum(local_counts, 'ctx')  20.5 us
    psum x1, blocking collectives, on_device(): lax.psum((jnp.sum(query_wide * query_wide, axis=1), jnp.sum(key_wide * ke...  15.1 us
    unnamed x20, local copies, waits for them, and re-layouts  13.6 us
    dot_general x3, matrix products, on_device(): jnp.einsum('qhd,khd->hqk', query_heads, key_view, preferred_element_type=...  4.46 us
  transfers between devices with their start and end apart: 2, of which 2 were waited for; matrix products, arithmetic and copies ran while one was open for 7% of the time, Pallas kernels for 0%

commit v1 on v0

v1 whole, which is shorter than its diff:
```python
import functools
import math

import jax
import jax.numpy as jnp
import numpy as np
from jax import lax
from jax.experimental import pallas as pl
from jax.experimental.pallas import tpu as pltpu
from jax.sharding import PartitionSpec as P

HD = 128
CLIPS = 4
EPSILON = 1e-06
NEGATIVE = -1e30
ROTARY_BASE = 10000.0
SIDE = 4
MESH = pl.DeviceIdType.MESH


def frequencies():
    p = HD // 6
    f = HD - 4 * p
    base = np.float32(ROTARY_BASE)
    first = np.float32(1.0) / base ** (np.arange(0, f, 2, dtype=np.float32) / np.float32(f))
    other = np.float32(1.0) / base ** (np.arange(0, 2 * p, 2, dtype=np.float32) / np.float32(2 * p))
    return np.repeat(np.concatenate([first, other, other]), 2)[None, :].astype(np.float32), f, f + 2 * p


def cols(h):
    if isinstance(h, int):
        return pl.ds(h * HD, HD)
    return pl.ds(pl.multiple_of(h * HD, HD), HD)


def kernel(
    rows_n, model, cut_a, cut_b,
    q, k, v, gq, gk, ids, freq, grid, out,
    pad, ssq_send, ssq_recv, cz_send, cz_recv, cx_send, cx_recv,
    krot, qrot, kh, vh, k4, v4, qh, q4, s_scr, o_send, o4_send, o4_recv, st_send, st_recv, starts_scr,
    sem_bs, sem_br, sem_zs, sem_zr, sem_xs, sem_xr, sem_os, sem_or,
):
    T = q.shape[0]
    me = lax.axis_index("ctx")
    row = lax.axis_index("row")
    x = me // SIDE
    z = lax.rem(me, SIDE)
    zs = [lax.rem(z + d, SIDE) for d in range(SIDE)]
    xs = [lax.rem(x + d, SIDE) for d in range(SIDE)]
    zpeer = [x * SIDE + a for a in zs]
    xpeer = [a * SIDE + z for a in xs]
    zsrc = [lax.rem(z + SIDE - d, SIDE) for d in range(SIDE)]
    xsrc = [lax.rem(x + SIDE - d, SIDE) for d in range(SIDE)]
    scale = 1.0 / math.sqrt(HD)

    barrier = pltpu.get_barrier_semaphore()
    for d in range(1, SIDE):
        pl.semaphore_signal(barrier, inc=1, device_id={"ctx": zpeer[d]}, device_id_type=MESH)
        pl.semaphore_signal(barrier, inc=1, device_id={"ctx": xpeer[d]}, device_id_type=MESH)
    for d in range(1, rows_n):
        pl.semaphore_signal(
            barrier, inc=1, device_id={"row": lax.rem(row + d, rows_n)}, device_id_type=MESH
        )

    sends = []

    def send(src, dst, ss, rs, where):
        c = pltpu.make_async_remote_copy(
            src_ref=src, dst_ref=dst, send_sem=ss, recv_sem=rs, device_id=where, device_id_type=MESH
        )
        c.start()
        sends.append(c)
        return c

    pad[T:, :] = jnp.zeros((pad.shape[0] - T, HD), jnp.float32)
    ssq_send[...] = jnp.zeros_like(ssq_send)
    for i, ref in enumerate((q, k)):
        acc = None
        for h in range(5):
            w = ref[:, h * HD : (h + 1) * HD].astype(jnp.float32)
            acc = w * w if acc is None else acc + w * w
        pad[:T, :] = acc
        ssq_send[i : i + 1, :] = jnp.sum(jnp.transpose(pad[...]), axis=0, keepdims=True)
    idrow = ids[...]
    level = lax.broadcasted_iota(jnp.int32, (8, T), 0)
    below = jnp.where(jnp.broadcast_to(idrow, (8, T)) < level, 1.0, 0.0).astype(jnp.float32)
    counts = jnp.broadcast_to(jnp.sum(below, axis=1, keepdims=True), (8, HD))
    cz_send[...] = counts

    pl.semaphore_wait(barrier, 2 * (SIDE - 1) + rows_n - 1)

    cz = [
        send(cz_send, cz_recv.at[d], sem_bs.at[d], sem_br.at[d], {"ctx": zpeer[d]})
        for d in range(1, SIDE)
    ]
    sq = [
        send(
            ssq_send, ssq_recv.at[d], sem_bs.at[8 + d], sem_br.at[8 + d],
            {"row": lax.rem(row + d, rows_n)},
        )
        for d in range(1, rows_n)
    ]

    def to_z(n, src, dst_own, dst_four):
        four = []
        own = []
        for d in (2, 1, 3):
            if dst_four is not None:
                four.append((d, send(
                    src.at[:, cols(4)], dst_four.at[z], sem_zs.at[n, 0, d], sem_zr.at[n, 0, d],
                    {"ctx": zpeer[d]},
                )))
        for d in (2, 1, 3):
            own.append((d, send(
                src.at[:, cols(zs[d])], dst_own, sem_zs.at[n, 1, d], sem_zr.at[n, 1, d],
                {"ctx": zpeer[d]},
            )))
        return dict(four), dict(own)

    def to_x(n, j, src, dst):
        return [
            send(src, dst, sem_xs.at[n, j, d], sem_xr.at[n, j, d], {"ctx": xpeer[d]})
            for d in (2, 1, 3)
        ]

    v_four, v_own = to_z(0, v, vh.at[me], v4)

    for c in cz:
        c.wait_recv()
    part = cz_send[...]
    for d in range(1, SIDE):
        part = part + cz_recv[d]
    cx_send[...] = part
    vx = [to_x(0, 0, v.at[:, cols(z)], vh.at[me])]
    vh[me] = v[:, cols(z)]
    v4[z] = v[:, cols(4)]
    cx = [
        send(cx_send, cx_recv.at[d], sem_bs.at[4 + d], sem_br.at[4 + d], {"ctx": xpeer[d]})
        for d in range(1, SIDE)
    ]
    for c in cx:
        c.wait_recv()
    starts = cx_send[...]
    for d in range(1, SIDE):
        starts = starts + cx_recv[d]
    starts_scr[...] = starts

    lane = lax.broadcasted_iota(jnp.int32, (T, HD), 1)
    token = (lax.broadcasted_iota(jnp.int32, (T, HD), 0) + me * T).astype(jnp.float32)
    first = jnp.zeros((T, HD), jnp.float32)
    height = jnp.full((T, HD), grid[0, 0].astype(jnp.float32))
    width = jnp.full((T, HD), grid[0, 1].astype(jnp.float32))
    for c in range(1, CLIPS):
        s = jnp.broadcast_to(starts[c : c + 1, :], (T, HD))
        inside = token >= s
        first = jnp.where(inside, s, first)
        height = jnp.where(inside, grid[c, 0].astype(jnp.float32), height)
        width = jnp.where(inside, grid[c, 1].astype(jnp.float32), width)
    offset = token - first
    frame = jnp.floor((offset + 0.5) / (height * width))
    lines = jnp.floor((offset + 0.5) / width)
    line = lines - height * jnp.floor((lines + 0.5) / height)
    column = offset - width * lines
    place = jnp.where(lane < cut_a, frame, jnp.where(lane < cut_b, line, column))
    angle = place * freq[...]
    cosine = jnp.cos(angle)
    even = lax.rem(lane, 2) == 0
    sine = jnp.sin(angle)

    for c in sq:
        c.wait_recv()
    total = ssq_send[...]
    for d in range(1, rows_n):
        total = total + ssq_recv[d]
    rs = lax.rsqrt(total / model + EPSILON)

    def rope(src, dst, gain, i):
        col = jnp.transpose(jnp.broadcast_to(rs[i : i + 1, :], (HD, rs.shape[1])))[:T, :]
        for h in (4, 0, 1, 2, 3):
            a = src[:, h * HD : (h + 1) * HD].astype(jnp.float32) * col
            a = a * gain[:, h * HD : (h + 1) * HD]
            partner = jnp.where(even, -pltpu.roll(a, HD - 1, 1), pltpu.roll(a, 1, 1))
            dst[:, h * HD : (h + 1) * HD] = (a * cosine + partner * sine).astype(jnp.bfloat16)

    rope(k, krot, gk, 1)
    kh[me] = krot[:, cols(z)]
    k4[z] = krot[:, cols(4)]
    k_four, k_own = to_z(1, krot, kh.at[me], k4)
    kx = [to_x(1, 0, krot.at[:, cols(z)], kh.at[me])]
    rope(q, qrot, gq, 0)
    qh[z] = qrot[:, cols(z)]
    q4[x] = qrot[:, cols(4)]
    q4s = [
        send(qrot.at[:, cols(4)], q4.at[x], sem_xs.at[2, 0, d], sem_xr.at[2, 0, d], {"ctx": xpeer[d]})
        for d in (2, 1, 3)
    ]
    _, q_own = to_z(2, qrot, qh.at[z], None)

    for j in (1, 3, 2):
        v_own[j].wait_recv()
        slot = vh.at[x * SIDE + zsrc[j]]
        vx.append(to_x(0, j, slot, slot))

    def clip_cols(first_token):
        t = (lax.broadcasted_iota(jnp.int32, (T, HD), 0) + first_token).astype(jnp.float32)
        c = jnp.zeros((T, HD), jnp.float32)
        for i in range(1, CLIPS):
            c = c + jnp.where(t >= starts_scr[i : i + 1, :], 1.0, 0.0)
        return c

    def clip_row(first_token):
        t = (lax.broadcasted_iota(jnp.int32, (1, wide), 1) + first_token).astype(jnp.float32)
        c = jnp.zeros((1, wide), jnp.float32)
        for i in range(1, CLIPS):
            edge = jnp.max(starts_scr[i : i + 1, :], axis=1, keepdims=True)
            c = c + jnp.where(t >= edge, 1.0, 0.0)
        return c

    wide = SIDE * T

    def attend(query, q_first, kref, vref, blocks, firsts):
        qc = clip_cols(q_first)[:, :1]
        peak = None
        for b in range(blocks):
            s = lax.dot_general(
                query, kref[SIDE * b : SIDE * b + SIDE].reshape(wide, HD), (((1,), (1,)), ((), ())),
                preferred_element_type=jnp.float32,
            )
            s = jnp.where(qc == clip_row(firsts(b)), s, NEGATIVE)
            s_scr[b] = s
            m = jnp.max(s, axis=1, keepdims=True)
            peak = m if peak is None else jnp.maximum(peak, m)
        summed = jnp.zeros((T, HD), jnp.float32)
        weight = jnp.zeros((T, 1), jnp.float32)
        for b in range(blocks):
            w = jnp.exp((s_scr[b] - peak) * scale)
            weight = weight + jnp.sum(w, axis=1, keepdims=True)
            summed = summed + jnp.dot(
                w.astype(jnp.bfloat16), vref[SIDE * b : SIDE * b + SIDE].reshape(wide, HD),
                preferred_element_type=jnp.float32,
            )
        return summed, weight, peak * scale

    for d in (1, 3, 2):
        v_four[d].wait_recv()
        k_four[d].wait_recv()
    for c in q4s:
        c.wait_recv()

    def four_body(i, carry):
        o, w, m = attend(q4[i], (i * SIDE + z) * T, k4, v4, 1, lambda b: x * wide)
        o4_send[i] = (o / w).astype(jnp.bfloat16)
        lanes = lax.broadcasted_iota(jnp.int32, (T, HD), 1)
        pad[:T, :] = jnp.where(lanes == 0, m, jnp.where(lanes == 1, w, 0.0))
        st_send[i] = jnp.transpose(pad[...])[:8, :]
        return carry

    lax.fori_loop(0, SIDE, four_body, 0)
    o4s = []
    for d in (2, 1, 3):
        o4s.append(send(
            o4_send.at[xs[d]], o4_recv.at[x], sem_os.at[0, d], sem_or.at[0, d], {"ctx": xpeer[d]}
        ))
        o4s.append(send(
            st_send.at[xs[d]], st_recv.at[x], sem_os.at[1, d], sem_or.at[1, d], {"ctx": xpeer[d]}
        ))

    for j in (1, 3, 2):
        k_own[j].wait_recv()
        slot = kh.at[x * SIDE + zsrc[j]]
        kx.append(to_x(1, j, slot, slot))
    for group in vx + kx:
        for c in group:
            c.wait_recv()

    backs = []
    for n in (2, 1, 3, 0):
        a = zs[n]
        if n:
            q_own[SIDE - n].wait_recv()
        o, w, _ = attend(qh[a], (x * SIDE + a) * T, kh, vh, SIDE, lambda b: b * wide)
        o = (o / w).astype(jnp.bfloat16)
        if n:
            o_send[n] = o
            backs.append(send(
                o_send.at[n], out.at[:, cols(z)], sem_os.at[2, n], sem_or.at[2, n], {"ctx": zpeer[n]}
            ))
        else:
            out[:, cols(z)] = o

    for c in o4s:
        c.wait_recv()
    o4_recv[x] = o4_send[x]
    st_recv[x] = st_send[x]
    means, totals, peaks = [], [], []
    for i in range(SIDE):
        pad128 = jnp.concatenate(
            [st_recv[i], jnp.zeros((HD - 8, st_recv.shape[2]), jnp.float32)], axis=0
        )
        st = jnp.transpose(pad128)[:T, :]
        peaks.append(st[:, 0:1])
        totals.append(st[:, 1:2])
    peak = functools.reduce(jnp.maximum, peaks)
    num = jnp.zeros((T, HD), jnp.float32)
    den = jnp.zeros((T, 1), jnp.float32)
    for i in range(SIDE):
        f = totals[i] * jnp.exp(peaks[i] - peak)
        den = den + f
        num = num + f * o4_recv[i].astype(jnp.float32)
    out[:, cols(4)] = (num / den).astype(jnp.bfloat16)

    for c in backs:
        c.wait_recv()
    for c in sends:
        c.wait_send()


def on_device(rows_n, queries, keys, values, gain_q, gain_k, clip_ids, clip_grid):
    T, width = queries.shape
    freq, cut_a, cut_b = frequencies()
    bf, f32 = jnp.bfloat16, jnp.float32
    vm = pl.BlockSpec(memory_space=pltpu.VMEM)
    dma = pltpu.SemaphoreType.DMA
    block = (T, HD)
    return pl.pallas_call(
        functools.partial(kernel, rows_n, float(width * rows_n), cut_a, cut_b),
        out_shape=jax.ShapeDtypeStruct((T, width), bf),
        in_specs=[vm] * 7 + [pl.BlockSpec(memory_space=pltpu.SMEM)],
        out_specs=vm,
        scratch_shapes=[
            pltpu.VMEM((256, HD), f32),
            pltpu.VMEM((8, 256), f32),
            pltpu.VMEM((rows_n, 8, 256), f32),
            pltpu.VMEM((8, HD), f32),
            pltpu.VMEM((SIDE, 8, HD), f32),
            pltpu.VMEM((8, HD), f32),
            pltpu.VMEM((SIDE, 8, HD), f32),
            pltpu.VMEM((T, width), bf),
            pltpu.VMEM((T, width), bf),
            pltpu.VMEM((SIDE * SIDE,) + block, bf),
            pltpu.VMEM((SIDE * SIDE,) + block, bf),
            pltpu.VMEM((SIDE,) + block, bf),
            pltpu.VMEM((SIDE,) + block, bf),
            pltpu.VMEM((SIDE,) + block, bf),
            pltpu.VMEM((SIDE,) + block, bf),
            pltpu.VMEM((SIDE, T, SIDE * T), f32),
            pltpu.VMEM((SIDE,) + block, bf),
            pltpu.VMEM((SIDE,) + block, bf),
            pltpu.VMEM((SIDE,) + block, bf),
            pltpu.VMEM((SIDE, 8, 256), f32),
            pltpu.VMEM((SIDE, 8, 256), f32),
            pltpu.VMEM((8, HD), f32),
            dma((16,)),
            dma((16,)),
            dma((3, 2, SIDE)),
            dma((3, 2, SIDE)),
            dma((3, SIDE, SIDE)),
            dma((3, SIDE, SIDE)),
            dma((3, SIDE)),
            dma((3, SIDE)),
        ],
        compiler_params=pltpu.CompilerParams(
            collective_id=0, has_side_effects=True, vmem_limit_bytes=48 * 1024 * 1024
        ),
        name="clip_attention",
    )(
        queries, keys, values, gain_q[None, :], gain_k[None, :], clip_ids[None, :],
        jnp.asarray(freq), clip_grid,
    )


def solution(mesh):
    in_specs = (
        P(("batch", "ctx"), "row"),
        P(("batch", "ctx"), "row"),
        P(("batch", "ctx"), "row"),
        P("row"),
        P("row"),
        P(("batch", "ctx")),
        P("batch", None),
    )
    out_specs = P(("batch", "ctx"), "row")
    return jax.shard_map(
        functools.partial(on_device, mesh.shape["row"]),
        mesh=mesh, in_specs=in_specs, out_specs=out_specs, check_vma=False,
    )
```

time: 214 us -> 62.5 us (0.29)
  the two profiles are of different devices: /device:TPU:1 before, /device:TPU:74 now
where the time goes in v1:
time: 62.5 us; the launch traced here: 62.2 us
  Pallas kernels  56.5 us (90%)
  local copies, waits for them, and re-layouts  5.67 us (9%)
    pallas_call x1, Pallas kernels, on_device(): pl.pallas_call(functools.partial(kernel, rows_n, float(width * rows_n), c...  56.5 us
    unnamed x16, local copies, waits for them, and re-layouts  5.67 us

profile of v1, /device:TPU:74, one launch (start us, length us, event | category | flops | bytes accessed | tf_op | source)
XLA Modules:
  0.0 62.2 jit_solution(1101441219001198120)
XLA Ops:
  0.0 0.0 copy-start.5
  0.0 0.8 %copy.9.grid = s32[4,2]{1,0:T(4,128)S(1)} copy(s32[4,2]{0,1:T(2,128)} %param.14) | data formatting | bytes 64 | tf_op args[6]
  0.8 0.0 copy-done.5
  0.8 0.0 copy-start.6
  0.8 0.7 %copy-done.6 = f32[640]{0:T(1024)S(1)} copy-done((f32[640]{0:T(1024)S(1)}, f32[640]{0:T(1024)}, u32[]{:S(2)}) %copy-start.6) | copy-done | bytes 2584
  1.5 0.0 copy-start.3
  1.5 0.0 copy-start.4
  1.5 0.7 %copy-done.3 = s32[192]{0:T(256)S(1)} copy-done((s32[192]{0:T(256)S(1)}, s32[192]{0:T(256)}, u32[]{:S(2)}) %copy-start.3) | copy-done | bytes 792
  2.2 0.0 copy-done.4
  2.2 0.0 copy-start
  2.2 0.9 %copy-done = bf16[192,640]{1,0:T(8,128)(2,1)S(1)} copy-done((bf16[192,640]{1,0:T(8,128)(2,1)S(1)}, bf16[192,640]{1,0:T(8,128)(2,1)}, u32[]{:S(2)}) %copy-start) | copy-done | bytes 245784
  3.1 0.0 copy-start.1
  3.1 0.9 %copy-done.1 = bf16[192,640]{1,0:T(8,128)(2,1)S(1)} copy-done((bf16[192,640]{1,0:T(8,128)(2,1)S(1)}, bf16[192,640]{1,0:T(8,128)(2,1)}, u32[]{:S(2)}) %copy-start.1) | copy-done | bytes 245784
  4.0 0.0 copy-start.2
  4.0 0.9 %copy-done.2 = bf16[192,640]{1,0:T(8,128)(2,1)S(1)} copy-done((bf16[192,640]{1,0:T(8,128)(2,1)S(1)}, bf16[192,640]{1,0:T(8,128)(2,1)}, u32[]{:S(2)}) %copy-start.2) | copy-done | bytes 245784
  5.0 56.5 %clip_attention.1 = bf16[192,640]{1,0:T(8,128)(2,1)S(1)} custom-call(bf16[192,640]{1,0:T(8,128)(2,1)S(1)} %copy-done, bf16[192,640]{1,0:T(8,128)(2,1)S(1)} %copy-done.1, bf16[192,640]{1,0:T(8,128)(2,1)S(1)} %copy-done.2, f32[1,640]{1,0:T(1,128)S(1)} %broadcast_in_dim.9.gq, f32[1,640]{1,0:T(1,128)S(1)} %broadcast_in_dim.10.gk, s32[1,192]{1,0:T(1,128)S(1)} %bitcast.1, ...), custom_call_target="tpu_custom_call" | custom-call | tf_op jit(solution)/shard_map/clip_attention/pallas_call | solution.py:325
  61.5 0.7 %copy.11 = bf16[192,640]{1,0:T(8,128)(2,1)} copy(bf16[192,640]{1,0:T(8,128)(2,1)S(1)} %clip_attention.1) | data formatting | bytes 491520
  (2 shorter events, 0.0 us)
Async XLA Ops:
  0.0 0.8 %copy-start.5 = (f32[640]{0:T(1024)S(1)}, f32[640]{0:T(1024)}, u32[]{:S(2)}) copy-start(f32[640]{0:T(1024)} %param.11) | copy-start | bytes 7684
  0.8 0.7 %copy-start.6 = (f32[640]{0:T(1024)S(1)}, f32[640]{0:T(1024)}, u32[]{:S(2)}) copy-start(f32[640]{0:T(1024)} %param.12) | copy-start | bytes 7684
  1.5 0.7 %copy-start.3 = (s32[192]{0:T(256)S(1)}, s32[192]{0:T(256)}, u32[]{:S(2)}) copy-start(s32[192]{0:T(256)} %param.13) | copy-start | bytes 2308
  1.5 0.7 %copy-start.4 = (f32[1,128]{1,0:T(1,128)S(1)}, f32[1,128]{1,0:T(1,128)}, u32[]{:S(2)}) copy-start(f32[1,128]{1,0:T(1,128)} %constant.2.clone.freq) | copy-start | bytes 1540
  2.2 0.9 %copy-start = (bf16[192,640]{1,0:T(8,128)(2,1)S(1)}, bf16[192,640]{1,0:T(8,128)(2,1)}, u32[]{:S(2)}) copy-start(bf16[192,640]{1,0:T(8,128)(2,1)} %q.1) | copy-start | bytes 737284
  3.1 0.9 %copy-start.1 = (bf16[192,640]{1,0:T(8,128)(2,1)S(1)}, bf16[192,640]{1,0:T(8,128)(2,1)}, u32[]{:S(2)}) copy-start(bf16[192,640]{1,0:T(8,128)(2,1)} %k.1) | copy-start | bytes 737284
  4.0 0.9 %copy-start.2 = (bf16[192,640]{1,0:T(8,128)(2,1)S(1)}, bf16[192,640]{1,0:T(8,128)(2,1)}, u32[]{:S(2)}) copy-start(bf16[192,640]{1,0:T(8,128)(2,1)} %v.1) | copy-start | bytes 737284

commit v2 on v1

v2 whole, which is shorter than its diff:
```python
import functools
import math

import jax
import jax.numpy as jnp
import numpy as np
from jax import lax
from jax.experimental import pallas as pl
from jax.experimental.pallas import tpu as pltpu
from jax.sharding import PartitionSpec as P

HD = 128
CLIPS = 4
EPSILON = 1e-06
NEGATIVE = -1e30
ROTARY_BASE = 10000.0
LOG2E = math.log2(math.e)
SIDE = 4
MESH = pl.DeviceIdType.MESH


def frequencies():
    p = HD // 6
    f = HD - 4 * p
    base = np.float32(ROTARY_BASE)
    first = np.float32(1.0) / base ** (np.arange(0, f, 2, dtype=np.float32) / np.float32(f))
    other = np.float32(1.0) / base ** (np.arange(0, 2 * p, 2, dtype=np.float32) / np.float32(2 * p))
    return np.repeat(np.concatenate([first, other, other]), 2)[None, :].astype(np.float32), f, f + 2 * p


def cols(h):
    if isinstance(h, int):
        return pl.ds(h * HD, HD)
    return pl.ds(pl.multiple_of(h * HD, HD), HD)


def kernel(
    rows_n, model, cut_a, cut_b,
    q_hbm, k_hbm, v, gq_hbm, gk_hbm, ids_hbm, freq_hbm, grid_hbm, out,
    q, k, gq, gk, ids, freq, grid, pad, ssq_send, ssq_recv, cz_send, cz_recv, cx_send, cx_recv,
    krot, qrot, kh, vh, k4, v4, qh, q4, m_scr, s_scr, a_scr, o_send, o4_send, o4_recv, st_send, st_recv, starts_scr,
    sem_s, sem_r, sem_zr, sem_xr, sem_in,
):
    T = q.shape[0]
    me = lax.axis_index("ctx")
    row = lax.axis_index("row")
    x = me // SIDE
    z = lax.rem(me, SIDE)
    zs = [lax.rem(z + d, SIDE) for d in range(SIDE)]
    xs = [lax.rem(x + d, SIDE) for d in range(SIDE)]
    zpeer = [x * SIDE + a for a in zs]
    xpeer = [a * SIDE + z for a in xs]
    zsrc = [lax.rem(z + SIDE - d, SIDE) for d in range(SIDE)]
    xsrc = [lax.rem(x + SIDE - d, SIDE) for d in range(SIDE)]
    scale = 1.0 / math.sqrt(HD)
    wide = SIDE * T

    def left(ref, i):
        return ref.at[i, :, 0:HD]

    barrier = pltpu.get_barrier_semaphore()
    for d in range(1, SIDE):
        pl.semaphore_signal(barrier, inc=1, device_id={"ctx": zpeer[d]}, device_id_type=MESH)
        pl.semaphore_signal(barrier, inc=1, device_id={"ctx": xpeer[d]}, device_id_type=MESH)
    for d in range(1, rows_n):
        pl.semaphore_signal(
            barrier, inc=1, device_id={"row": lax.rem(row + d, rows_n)}, device_id_type=MESH
        )
    loads = [
        pltpu.make_async_copy(src, dst, sem_in.at[i])
        for i, (src, dst) in enumerate([
            (ids_hbm, ids), (q_hbm, q), (k_hbm, k), (grid_hbm, grid), (freq_hbm, freq),
            (gk_hbm, gk), (gq_hbm, gq), (v.at[:, cols(z)], left(vh, z)), (v.at[:, cols(4)], left(v4, z)),
        ])
    ]
    for c in loads:
        c.start()

    def send(src, dst, group, arrival, where):
        pltpu.make_async_remote_copy(
            src_ref=src, dst_ref=dst, send_sem=sem_s.at[group], recv_sem=arrival, device_id=where,
            device_id_type=MESH,
        ).start()

    def done(ref, sem):
        pltpu.make_async_copy(ref, ref, sem).wait()

    def to_z(n, src, dst):
        for d in (1, 3, 2):
            send(src.at[:, cols(zs[d])], dst, 2 + n, sem_zr.at[n, d], {"ctx": zpeer[d]})

    def four_to_z(n, src, dst):
        for d in (1, 3, 2):
            send(src.at[:, cols(4)], left(dst, z), 2 + n, sem_r.at[n], {"ctx": zpeer[d]})

    def to_x(n, src, dst, a):
        for d in (1, 3, 2):
            send(src, left(dst, d * SIDE + a), n, sem_xr.at[n], {"ctx": xpeer[d]})

    loads[0].wait()
    level = lax.broadcasted_iota(jnp.int32, (8, T), 0)
    below = jnp.where(jnp.broadcast_to(ids[...], (8, T)) < level, 1.0, 0.0).astype(jnp.float32)
    cz_send[...] = jnp.broadcast_to(jnp.sum(below, axis=1, keepdims=True), (8, HD))

    with jax.named_scope("entry_wait"):
        pl.semaphore_wait(barrier, 2 * (SIDE - 1) + rows_n - 1)

    for d in range(1, SIDE):
        send(cz_send, cz_recv.at[d], 6, sem_r.at[3], {"ctx": zpeer[d]})
    to_z(0, v, left(vh, z))
    to_x(0, v.at[:, cols(z)], vh, z)
    four_to_z(0, v, v4)

    with jax.named_scope("squares"):
        pad[T:256, :] = jnp.zeros((256 - T, HD), jnp.float32)
        ssq_send[...] = jnp.zeros_like(ssq_send)
        for i, ref in enumerate((q, k)):
            loads[1 + i].wait()
            acc = None
            for h in range(5):
                w = ref[:, h * HD : (h + 1) * HD].astype(jnp.float32)
                acc = w * w if acc is None else acc + w * w
            pad[:T, :] = acc
            ssq_send[i : i + 1, :] = jnp.sum(jnp.transpose(pad[0:256, :]), axis=0, keepdims=True)
    for d in range(1, rows_n):
        send(
            ssq_send, ssq_recv.at[d], 7, sem_r.at[5], {"row": lax.rem(row + d, rows_n)}
        )

    with jax.named_scope("count_z_wait"):
        done(cz_recv.at[1:SIDE], sem_r.at[3])
    part = cz_send[...]
    for d in range(1, SIDE):
        part = part + cz_recv[d]
    cx_send[...] = part
    for d in range(1, SIDE):
        send(cx_send, cx_recv.at[d], 6, sem_r.at[4], {"ctx": xpeer[d]})

    def forward(n, ref, j):
        slot = left(ref, zsrc[j])
        with jax.named_scope("%s_wait%d" % ("vk"[n], j)):
            done(slot, sem_zr.at[n, j])
        to_x(n, slot, ref, zsrc[j])

    forward(0, vh, 1)
    forward(0, vh, 3)
    with jax.named_scope("count_x_wait"):
        done(cx_recv.at[1:SIDE], sem_r.at[4])
    starts = cx_send[...]
    for d in range(1, SIDE):
        starts = starts + cx_recv[d]
    starts_scr[...] = starts

    for c in loads[3:]:
        c.wait()
    lane = lax.broadcasted_iota(jnp.int32, (T, HD), 1)
    token = (lax.broadcasted_iota(jnp.int32, (T, HD), 0) + me * T).astype(jnp.float32)
    first = jnp.zeros((T, HD), jnp.float32)
    shape_of = grid[...].astype(jnp.float32)
    height = jnp.broadcast_to(shape_of[0:1, 0:1], (T, HD))
    width = jnp.broadcast_to(shape_of[1:2, 0:1], (T, HD))
    for c in range(1, CLIPS):
        s = jnp.broadcast_to(starts[c : c + 1, :], (T, HD))
        inside = token >= s
        first = jnp.where(inside, s, first)
        height = jnp.where(inside, shape_of[0:1, c : c + 1], height)
        width = jnp.where(inside, shape_of[1:2, c : c + 1], width)
    offset = token - first
    frame = jnp.floor((offset + 0.5) / (height * width))
    lines = jnp.floor((offset + 0.5) / width)
    line = lines - height * jnp.floor((lines + 0.5) / height)
    column = offset - width * lines
    place = jnp.where(lane < cut_a, frame, jnp.where(lane < cut_b, line, column))
    angle = place * freq[...]
    with jax.named_scope("trig"):
        cosine = jnp.cos(angle)
    even = lax.rem(lane, 2) == 0
    sine = jnp.sin(angle)

    with jax.named_scope("square_wait"):
        if rows_n > 1:
            done(ssq_recv.at[1:rows_n], sem_r.at[5])
    total = ssq_send[...]
    for d in range(1, rows_n):
        total = total + ssq_recv[d]
    rs = lax.rsqrt(total / model + EPSILON)

    def rope(src, dst, gain, i):
        col = jnp.transpose(jnp.broadcast_to(rs[i : i + 1, :], (HD, rs.shape[1])))[:T, :]
        for h in (4, 0, 1, 2, 3):
            a = src[:, h * HD : (h + 1) * HD].astype(jnp.float32) * col
            a = a * gain[h * HD : (h + 1) * HD].reshape(1, HD)
            partner = jnp.where(even, -pltpu.roll(a, HD - 1, 1), pltpu.roll(a, 1, 1))
            dst[:, h * HD : (h + 1) * HD] = (a * cosine + partner * sine).astype(jnp.bfloat16)

    with jax.named_scope("rope_k"):
        rope(k, krot, gk, 1)
    to_z(1, krot, left(kh, z))
    to_x(1, krot.at[:, cols(z)], kh, z)
    forward(0, vh, 2)
    with jax.named_scope("rope_q"):
        rope(q, qrot, gq, 0)
    for d in (1, 3, 2):
        send(qrot.at[:, cols(zs[d])], left(qh, z), 4, sem_zr.at[2, d], {"ctx": zpeer[d]})
    four_to_z(1, krot, k4)
    kh[z, :, 0:HD] = krot[:, cols(z)]
    k4[z, :, 0:HD] = krot[:, cols(4)]
    qh[z, :, 0:HD] = qrot[:, cols(z)]
    q4[x, :, 0:HD] = qrot[:, cols(4)]

    lanes = lax.broadcasted_iota(jnp.int32, (T, HD), 1)

    def member(first_token, inside, outside):
        t = (lax.broadcasted_iota(jnp.int32, (T, HD), 0) + first_token).astype(jnp.float32)
        c = jnp.zeros((T, HD), jnp.int32)
        for i in range(1, CLIPS):
            c = c + jnp.where(t >= starts_scr[i : i + 1, :], 1, 0)
        value = jnp.where(c == lanes, inside, outside)
        return jnp.where(lanes < CLIPS, value, 0.0).astype(jnp.bfloat16)

    ones = jnp.ones((T, HD), jnp.bfloat16)

    def fill(i, carry):
        vh[i, :, HD:] = ones
        block = lax.rem(x + SIDE - i // SIDE, SIDE) * SIDE + lax.rem(i, SIDE)
        kh[i, :, HD:] = member(block * T, 1.0, 0.0)
        return carry

    def fill_four(i, carry):
        v4[i, :, HD:] = ones
        k4[i, :, HD:] = member((x * SIDE + i) * T, 1.0, 0.0)
        qh[i, :, HD:] = member((x * SIDE + i) * T, 0.0, NEGATIVE)
        q4[i, :, HD:] = member((i * SIDE + z) * T, 0.0, NEGATIVE)
        return carry

    with jax.named_scope("fill"):
        lax.fori_loop(0, SIDE, fill_four, 0)
        lax.fori_loop(0, SIDE * SIDE, fill, 0)
    for j in (1, 3, 2):
        forward(1, kh, j)
    for d in (1, 3, 2):
        send(qrot.at[:, cols(4)], left(q4, x), 4, sem_r.at[2], {"ctx": xpeer[d]})

    third = wide // 3

    def attend(queries, keys, vals, carried=None):
        keys = keys.reshape(-1, 2 * HD)
        vals = vals.reshape(-1, 2 * HD)
        n = keys.shape[0]
        for t in range(3):
            tile = pl.ds(t * third, third)
            s = lax.dot_general(
                queries[t * third : (t + 1) * third], keys, (((1,), (1,)), ((), ())),
                preferred_element_type=jnp.float32,
            )
            s_scr[t, :, 0:n] = s
            m = jnp.max(s, axis=1, keepdims=True)
            if carried:
                old = m_scr[tile, 0:1]
                m = jnp.maximum(m, old)
                factor = jnp.exp2((old - m) * (scale * LOG2E))
            w = jnp.exp2((s_scr[t, :, 0:n] - m) * (scale * LOG2E)).astype(jnp.bfloat16)
            o = jnp.dot(w, vals, preferred_element_type=jnp.float32)
            if carried:
                o = o + a_scr[tile, :] * factor
            a_scr[tile, :] = o
            m_scr[tile, :] = jnp.broadcast_to(m, (third, HD))

    def divide(o):
        return (o[:, :HD] / o[:, HD:]).astype(jnp.bfloat16)

    with jax.named_scope("q_wait"):
        for n in (3, 1, 2):
            done(left(qh, zs[n]), sem_zr.at[2, SIDE - n])
    with jax.named_scope("own_attend"):
        attend(qh[...].reshape(wide, 2 * HD), kh[0:SIDE], vh[0:SIDE])
    with jax.named_scope("x_wait"):
        done(left(vh, pl.ds(SIDE, 3 * SIDE)), sem_xr.at[0])
        done(left(kh, pl.ds(SIDE, 3 * SIDE)), sem_xr.at[1])
    with jax.named_scope("x_attend"):
        attend(qh[...].reshape(wide, 2 * HD), kh[SIDE:], vh[SIDE:], True)
        o_send[...] = divide(a_scr[...]).reshape(SIDE, T, HD)
    for n in (2, 1, 3):
        send(o_send.at[zs[n]], out.at[:, cols(z)], 5, sem_r.at[6], {"ctx": zpeer[n]})
    out[:, cols(z)] = o_send[z]

    with jax.named_scope("four_wait"):
        done(left(v4, pl.ds(0, SIDE - 1)), sem_r.at[0])
        done(left(k4, pl.ds(0, SIDE - 1)), sem_r.at[1])
        done(left(q4, pl.ds(0, SIDE - 1)), sem_r.at[2])
    with jax.named_scope("four_attend"):
        pad[wide:, :] = jnp.zeros((64, HD), jnp.float32)
        attend(q4[...].reshape(wide, 2 * HD), k4[...], v4[...])
        m, o = m_scr[...], a_scr[...]
        o4_send[...] = divide(o).reshape(SIDE, T, HD)
        flags = lax.broadcasted_iota(jnp.int32, (wide, HD), 1)
        pad[0:wide, :] = jnp.where(flags == 0, m * scale, jnp.where(flags == 1, o[:, HD:], 0.0))
        for i in range(SIDE):
            st_send[i] = jnp.transpose(pad[i * T : i * T + 256, :])[:8, :]
    for d in (1, 3, 2):
        send(o4_send.at[xs[d]], o4_recv.at[x], 5, sem_r.at[7], {"ctx": xpeer[d]})
        send(st_send.at[xs[d]], st_recv.at[x], 8, sem_r.at[8], {"ctx": xpeer[d]})
    o4_recv[x] = o4_send[x]
    st_recv[x] = st_send[x]
    with jax.named_scope("four_back_wait"):
        done(o4_recv.at[0 : SIDE - 1], sem_r.at[7])
        done(st_recv.at[0 : SIDE - 1], sem_r.at[8])
    totals, peaks = [], []
    for i in range(SIDE):
        pad128 = jnp.concatenate(
            [st_recv[i], jnp.zeros((HD - 8, st_recv.shape[2]), jnp.float32)], axis=0
        )
        st = jnp.transpose(pad128)[:T, :]
        peaks.append(st[:, 0:1])
        totals.append(st[:, 1:2])
    peak = functools.reduce(jnp.maximum, peaks)
    num = jnp.zeros((T, HD), jnp.float32)
    den = jnp.zeros((T, 1), jnp.float32)
    for i in range(SIDE):
        f = totals[i] * jnp.exp(peaks[i] - peak)
        den = den + f
        num = num + f * o4_recv[i].astype(jnp.float32)
    out[:, cols(4)] = (num / den).astype(jnp.bfloat16)

    with jax.named_scope("back_wait"):
        done(o4_recv.at[0 : SIDE - 1], sem_r.at[6])
    with jax.named_scope("send_wait"):
        done(left(vh, pl.ds(0, 3 * SIDE)), sem_s.at[0])
        done(left(kh, pl.ds(0, 3 * SIDE)), sem_s.at[1])
        for group in range(2, 6):
            done(left(vh, pl.ds(0, 6)), sem_s.at[group])
        done(st_recv.at[0 : SIDE - 1], sem_s.at[6])
        if rows_n > 1:
            done(ssq_recv.at[1:rows_n], sem_s.at[7])
        done(st_recv.at[0 : SIDE - 1], sem_s.at[8])


def on_device(rows_n, queries, keys, values, gain_q, gain_k, clip_ids, clip_grid):
    T, width = queries.shape
    freq, cut_a, cut_b = frequencies()
    bf, f32 = jnp.bfloat16, jnp.float32
    vm = pl.BlockSpec(memory_space=pltpu.VMEM)
    dma = pltpu.SemaphoreType.DMA
    block = (T, HD)
    return pl.pallas_call(
        functools.partial(kernel, rows_n, float(width * rows_n), cut_a, cut_b),
        out_shape=pltpu.VMEM((T, width), bf),
        in_specs=[pl.BlockSpec(memory_space=pltpu.HBM)] * 8,
        out_specs=vm,
        scratch_shapes=[
            pltpu.VMEM((T, width), bf),
            pltpu.VMEM((T, width), bf),
            pltpu.VMEM((width,), f32),
            pltpu.VMEM((width,), f32),
            pltpu.VMEM((1, T), jnp.int32),
            pltpu.VMEM((1, HD), f32),
            pltpu.VMEM((2, CLIPS), jnp.int32),
            pltpu.VMEM((SIDE * T + 64, HD), f32),
            pltpu.VMEM((8, 256), f32),
            pltpu.VMEM((rows_n, 8, 256), f32),
            pltpu.VMEM((8, HD), f32),
            pltpu.VMEM((SIDE, 8, HD), f32),
            pltpu.VMEM((8, HD), f32),
            pltpu.VMEM((SIDE, 8, HD), f32),
            pltpu.VMEM((T, width), bf),
            pltpu.VMEM((T, width), bf),
            pltpu.VMEM((SIDE * SIDE, T, 2 * HD), bf),
            pltpu.VMEM((SIDE * SIDE, T, 2 * HD), bf),
            pltpu.VMEM((SIDE, T, 2 * HD), bf),
            pltpu.VMEM((SIDE, T, 2 * HD), bf),
            pltpu.VMEM((SIDE, T, 2 * HD), bf),
            pltpu.VMEM((SIDE, T, 2 * HD), bf),
            pltpu.VMEM((SIDE * T, HD), f32),
            pltpu.VMEM((3, SIDE * T // 3, 3 * SIDE * T), f32),
            pltpu.VMEM((SIDE * T, 2 * HD), f32),
            pltpu.VMEM((SIDE,) + block, bf),
            pltpu.VMEM((SIDE,) + block, bf),
            pltpu.VMEM((SIDE,) + block, bf),
            pltpu.VMEM((SIDE, 8, 256), f32),
            pltpu.VMEM((SIDE, 8, 256), f32),
            pltpu.VMEM((8, HD), f32),
            dma((9,)),
            dma((9,)),
            dma((3, SIDE)),
            dma((2,)),
            dma((9,)),
        ],
        compiler_params=pltpu.CompilerParams(
            collective_id=0, has_side_effects=True, vmem_limit_bytes=48 * 1024 * 1024
        ),
        name="clip_attention",
    )(*[pltpu.with_memory_space_constraint(a, pltpu.HBM) for a in (
        queries, keys, values, gain_q, gain_k, clip_ids[None, :], jnp.asarray(freq), clip_grid.T,
    )])


def solution(mesh):
    in_specs = (
        P(("batch", "ctx"), "row"),
        P(("batch", "ctx"), "row"),
        P(("batch", "ctx"), "row"),
        P("row"),
        P("row"),
        P(("batch", "ctx")),
        P("batch", None),
    )
    out_specs = P(("batch", "ctx"), "row")
    return jax.shard_map(
        functools.partial(on_device, mesh.shape["row"]),
        mesh=mesh, in_specs=in_specs, out_specs=out_specs, check_vma=False,
    )
```

time: 62.5 us -> 54.7 us (0.88)
  the two profiles are of different devices: /device:TPU:74 before, /device:TPU:68 now
where the time goes in v2:
time: 54.7 us; the launch traced here: 54.5 us
  Pallas kernels  53.8 us (98%)
  local copies, waits for them, and re-layouts  0.7 us (1%)
    pallas_call x1, Pallas kernels, on_device(): pl.pallas_call(functools.partial(kernel, rows_n, float(width * rows_n), c...  53.8 us

profile of v2, /device:TPU:68, one launch (start us, length us, event | category | flops | bytes accessed | tf_op | source)
XLA Modules:
  0.0 54.5 jit_solution(5060583215098036395)
XLA Ops:
  0.0 53.8 %clip_attention.1 = bf16[192,640]{1,0:T(8,128)(2,1)S(1)} custom-call(bf16[192,640]{1,0:T(8,128)(2,1)} %q_hbm.1, bf16[192,640]{1,0:T(8,128)(2,1)} %k_hbm.1, bf16[192,640]{1,0:T(8,128)(2,1)} %v.1, f32[640]{0:T(1024)} %gq_hbm.1, f32[640]{0:T(1024)} %gk_hbm.1, s32[1,192]{1,0:T(1,128)} %bitcast.2, f32[1,128]{1,0:T(1,128)} %constant.2.clone.freq_hbm, s32[2,4]{1,0:T(2,128)} %bitcast.3), custom_call_target="tpu_custom_call" | custom-call | tf_op jit(solution)/shard_map/clip_attention/pallas_call | solution.py:345
  53.8 0.7 %copy.10 = bf16[192,640]{1,0:T(8,128)(2,1)} copy(bf16[192,640]{1,0:T(8,128)(2,1)S(1)} %clip_attention.1) | data formatting | bytes 491520

commit v3 on v2

--- a/solution.py
+++ b/solution.py
@@ -93,9 +93,12 @@
         for d in (1, 3, 2):
             send(src.at[:, cols(4)], left(dst, z), 2 + n, sem_r.at[n], {"ctx": zpeer[d]})
 
-    def to_x(n, src, dst, a):
-        for d in (1, 3, 2):
-            send(src, left(dst, d * SIDE + a), n, sem_xr.at[n], {"ctx": xpeer[d]})
+    def to_near(n, src, dst, a):
+        for g, d in ((1, 1), (2, 3)):
+            send(src, left(dst, g * SIDE + a), n, sem_xr.at[n, 0], {"ctx": xpeer[d]})
+
+    def to_far(n, src, dst, a):
+        send(src, left(dst, 3 * SIDE + a), n, sem_xr.at[n, 1], {"ctx": xpeer[2]})
 
     loads[0].wait()
     level = lax.broadcasted_iota(jnp.int32, (8, T), 0)
@@ -108,8 +111,8 @@
     for d in range(1, SIDE):
         send(cz_send, cz_recv.at[d], 6, sem_r.at[3], {"ctx": zpeer[d]})
     to_z(0, v, left(vh, z))
-    to_x(0, v.at[:, cols(z)], vh, z)
-    four_to_z(0, v, v4)
+    to_near(0, v.at[:, cols(z)], vh, z)
+    to_far(0, v.at[:, cols(z)], vh, z)
 
     with jax.named_scope("squares"):
         pad[T:256, :] = jnp.zeros((256 - T, HD), jnp.float32)
@@ -140,8 +143,11 @@
         slot = left(ref, zsrc[j])
         with jax.named_scope("%s_wait%d" % ("vk"[n], j)):
             done(slot, sem_zr.at[n, j])
-        to_x(n, slot, ref, zsrc[j])
-
+        to_near(n, slot, ref, zsrc[j])
+        if n == 0:
+            to_far(n, slot, ref, zsrc[j])
+
+    four_to_z(0, v, v4)
     forward(0, vh, 1)
     forward(0, vh, 3)
     with jax.named_scope("count_x_wait"):
@@ -196,13 +202,13 @@
     with jax.named_scope("rope_k"):
         rope(k, krot, gk, 1)
     to_z(1, krot, left(kh, z))
-    to_x(1, krot.at[:, cols(z)], kh, z)
+    to_near(1, krot.at[:, cols(z)], kh, z)
+    to_far(1, krot.at[:, cols(z)], kh, z)
     forward(0, vh, 2)
     with jax.named_scope("rope_q"):
         rope(q, qrot, gq, 0)
     for d in (1, 3, 2):
         send(qrot.at[:, cols(zs[d])], left(qh, z), 4, sem_zr.at[2, d], {"ctx": zpeer[d]})
-    four_to_z(1, krot, k4)
     kh[z, :, 0:HD] = krot[:, cols(z)]
     k4[z, :, 0:HD] = krot[:, cols(4)]
     qh[z, :, 0:HD] = qrot[:, cols(z)]
@@ -220,11 +226,13 @@
 
     ones = jnp.ones((T, HD), jnp.bfloat16)
 
-    def fill(i, carry):
-        vh[i, :, HD:] = ones
-        block = lax.rem(x + SIDE - i // SIDE, SIDE) * SIDE + lax.rem(i, SIDE)
-        kh[i, :, HD:] = member(block * T, 1.0, 0.0)
-        return carry
+    def fill(g, d):
+        def body(i, carry):
+            vh[g * SIDE + i, :, HD:] = ones
+            kh[g * SIDE + i, :, HD:] = member((xsrc[d] * SIDE + i) * T, 1.0, 0.0)
+            return carry
+
+        lax.fori_loop(0, SIDE, body, 0)
 
     def fill_four(i, carry):
         v4[i, :, HD:] = ones
@@ -235,9 +243,12 @@
 
     with jax.named_scope("fill"):
         lax.fori_loop(0, SIDE, fill_four, 0)
-        lax.fori_loop(0, SIDE * SIDE, fill, 0)
+        for g, d in enumerate((0, 1, 3, 2)):
+            fill(g, d)
     for j in (1, 3, 2):
         forward(1, kh, j)
+    for j in (1, 3, 2):
+        to_far(1, left(kh, zsrc[j]), kh, zsrc[j])
     for d in (1, 3, 2):
         send(qrot.at[:, cols(4)], left(q4, x), 4, sem_r.at[2], {"ctx": xpeer[d]})
 
@@ -272,13 +283,17 @@
     with jax.named_scope("q_wait"):
         for n in (3, 1, 2):
             done(left(qh, zs[n]), sem_zr.at[2, SIDE - n])
+    four_to_z(1, krot, k4)
     with jax.named_scope("own_attend"):
         attend(qh[...].reshape(wide, 2 * HD), kh[0:SIDE], vh[0:SIDE])
-    with jax.named_scope("x_wait"):
-        done(left(vh, pl.ds(SIDE, 3 * SIDE)), sem_xr.at[0])
-        done(left(kh, pl.ds(SIDE, 3 * SIDE)), sem_xr.at[1])
-    with jax.named_scope("x_attend"):
-        attend(qh[...].reshape(wide, 2 * HD), kh[SIDE:], vh[SIDE:], True)
+    queries = qh[...].reshape(wide, 2 * HD)
+    for name, side, first, last in (("near", 0, SIDE, 3 * SIDE), ("far", 1, 3 * SIDE, 4 * SIDE)):
+        with jax.named_scope(name + "_wait"):
+            done(left(vh, pl.ds(first, last - first)), sem_xr.at[0, side])
+            done(left(kh, pl.ds(first, last - first)), sem_xr.at[1, side])
+        with jax.named_scope(name + "_attend"):
+            attend(queries, kh[first:last], vh[first:last], True)
+    with jax.named_scope("divide"):
         o_send[...] = divide(a_scr[...]).reshape(SIDE, T, HD)
     for n in (2, 1, 3):
         send(o_send.at[zs[n]], out.at[:, cols(z)], 5, sem_r.at[6], {"ctx": zpeer[n]})
@@ -305,22 +320,19 @@
     with jax.named_scope("four_back_wait"):
         done(o4_recv.at[0 : SIDE - 1], sem_r.at[7])
         done(st_recv.at[0 : SIDE - 1], sem_r.at[8])
-    totals, peaks = [], []
+    peaks = [st_recv[i, 0:1, :] for i in range(SIDE)]
+    peak = functools.reduce(jnp.maximum, peaks)
+    shares = [st_recv[i, 1:2, :] * jnp.exp(peaks[i] - peak) for i in range(SIDE)]
+    whole = functools.reduce(jnp.add, shares)
+    line = lax.broadcasted_iota(jnp.int32, (HD, st_recv.shape[2]), 0)
+    table = jnp.zeros((HD, st_recv.shape[2]), jnp.float32)
     for i in range(SIDE):
-        pad128 = jnp.concatenate(
-            [st_recv[i], jnp.zeros((HD - 8, st_recv.shape[2]), jnp.float32)], axis=0
-        )
-        st = jnp.transpose(pad128)[:T, :]
-        peaks.append(st[:, 0:1])
-        totals.append(st[:, 1:2])
-    peak = functools.reduce(jnp.maximum, peaks)
+        table = jnp.where(line == i, shares[i] / whole, table)
+    share = jnp.transpose(table)[:T, :]
     num = jnp.zeros((T, HD), jnp.float32)
-    den = jnp.zeros((T, 1), jnp.float32)
     for i in range(SIDE):
-        f = totals[i] * jnp.exp(peaks[i] - peak)
-        den = den + f
-        num = num + f * o4_recv[i].astype(jnp.float32)
-    out[:, cols(4)] = (num / den).astype(jnp.bfloat16)
+        num = num + share[:, i : i + 1] * o4_recv[i].astype(jnp.float32)
+    out[:, cols(4)] = num.astype(jnp.bfloat16)
 
     with jax.named_scope("back_wait"):
         done(o4_recv.at[0 : SIDE - 1], sem_r.at[6])
@@ -371,7 +383,7 @@
             pltpu.VMEM((SIDE, T, 2 * HD), bf),
             pltpu.VMEM((SIDE, T, 2 * HD), bf),
             pltpu.VMEM((SIDE * T, HD), f32),
-            pltpu.VMEM((3, SIDE * T // 3, 3 * SIDE * T), f32),
+            pltpu.VMEM((3, SIDE * T // 3, 2 * SIDE * T), f32),
             pltpu.VMEM((SIDE * T, 2 * HD), f32),
             pltpu.VMEM((SIDE,) + block, bf),
             pltpu.VMEM((SIDE,) + block, bf),
@@ -382,7 +394,7 @@
             dma((9,)),
             dma((9,)),
             dma((3, SIDE)),
-            dma((2,)),
+            dma((2, 2)),
             dma((9,)),
         ],
         compiler_params=pltpu.CompilerParams(

time: 54.7 us -> 48.9 us (0.89)
  the two profiles are of different devices: /device:TPU:68 before, /device:TPU:72 now
where the time goes in v3:
time: 48.9 us; the launch traced here: 48.8 us
  Pallas kernels  48.1 us (98%)
  local copies, waits for them, and re-layouts  0.7 us (1%)
    pallas_call x1, Pallas kernels, on_device(): pl.pallas_call(functools.partial(kernel, rows_n, float(width * rows_n), c...  48.1 us

profile of v3, /device:TPU:72, one launch (start us, length us, event | category | flops | bytes accessed | tf_op | source)
XLA Modules:
  0.0 48.8 jit_solution(11060529758270887487)
XLA Ops:
  0.0 48.1 %clip_attention.1 = bf16[192,640]{1,0:T(8,128)(2,1)S(1)} custom-call(bf16[192,640]{1,0:T(8,128)(2,1)} %q_hbm.1, bf16[192,640]{1,0:T(8,128)(2,1)} %k_hbm.1, bf16[192,640]{1,0:T(8,128)(2,1)} %v.1, f32[640]{0:T(1024)} %gq_hbm.1, f32[640]{0:T(1024)} %gk_hbm.1, s32[1,192]{1,0:T(1,128)} %bitcast.2, f32[1,128]{1,0:T(1,128)} %constant.2.clone.freq_hbm, s32[2,4]{1,0:T(2,128)} %bitcast.3), custom_call_target="tpu_custom_call" | custom-call | tf_op jit(solution)/shard_map/clip_attention/pallas_call | solution.py:357
  48.1 0.7 %copy.10 = bf16[192,640]{1,0:T(8,128)(2,1)} copy(bf16[192,640]{1,0:T(8,128)(2,1)S(1)} %clip_attention.1) | data formatting | bytes 491520

commit v4 on v3

--- a/solution.py
+++ b/solution.py
@@ -58,6 +58,14 @@
     def left(ref, i):
         return ref.at[i, :, 0:HD]
 
+    loads = [
+        pltpu.make_async_copy(src, dst, sem_in.at[i])
+        for i, (src, dst) in enumerate([
+            (ids_hbm, ids), (q_hbm, q), (k_hbm, k), (grid_hbm, grid), (freq_hbm, freq),
+            (gk_hbm, gk), (gq_hbm, gq), (v.at[:, cols(z)], left(vh, z)), (v.at[:, cols(4)], left(v4, z)),
+        ])
+    ]
+    loads[0].start()
     barrier = pltpu.get_barrier_semaphore()
     for d in range(1, SIDE):
         pl.semaphore_signal(barrier, inc=1, device_id={"ctx": zpeer[d]}, device_id_type=MESH)
@@ -66,14 +74,7 @@
         pl.semaphore_signal(
             barrier, inc=1, device_id={"row": lax.rem(row + d, rows_n)}, device_id_type=MESH
         )
-    loads = [
-        pltpu.make_async_copy(src, dst, sem_in.at[i])
-        for i, (src, dst) in enumerate([
-            (ids_hbm, ids), (q_hbm, q), (k_hbm, k), (grid_hbm, grid), (freq_hbm, freq),
-            (gk_hbm, gk), (gq_hbm, gq), (v.at[:, cols(z)], left(vh, z)), (v.at[:, cols(4)], left(v4, z)),
-        ])
-    ]
-    for c in loads:
+    for c in loads[1:]:
         c.start()
 
     def send(src, dst, group, arrival, where):
@@ -306,14 +307,17 @@
     with jax.named_scope("four_attend"):
         pad[wide:, :] = jnp.zeros((64, HD), jnp.float32)
         attend(q4[...].reshape(wide, 2 * HD), k4[...], v4[...])
-        m, o = m_scr[...], a_scr[...]
-        o4_send[...] = divide(o).reshape(SIDE, T, HD)
+        o4_send[...] = divide(a_scr[...]).reshape(SIDE, T, HD)
+    for d in (2, 1, 3):
+        send(o4_send.at[xs[d]], o4_recv.at[x], 5, sem_r.at[7], {"ctx": xpeer[d]})
+    with jax.named_scope("stats"):
         flags = lax.broadcasted_iota(jnp.int32, (wide, HD), 1)
-        pad[0:wide, :] = jnp.where(flags == 0, m * scale, jnp.where(flags == 1, o[:, HD:], 0.0))
+        pad[0:wide, :] = jnp.where(
+            flags == 0, m_scr[...] * scale, jnp.where(flags == 1, a_scr[:, HD:], 0.0)
+        )
         for i in range(SIDE):
             st_send[i] = jnp.transpose(pad[i * T : i * T + 256, :])[:8, :]
-    for d in (1, 3, 2):
-        send(o4_send.at[xs[d]], o4_recv.at[x], 5, sem_r.at[7], {"ctx": xpeer[d]})
+    for d in (2, 1, 3):
         send(st_send.at[xs[d]], st_recv.at[x], 8, sem_r.at[8], {"ctx": xpeer[d]})
     o4_recv[x] = o4_send[x]
     st_recv[x] = st_send[x]

time: 48.9 us -> 48.8 us (level)
  no operation moved by 1% of the time
where the time goes in v4:
time: 48.8 us; the launch traced here: 48.7 us
  Pallas kernels  48 us (98%)
  local copies, waits for them, and re-layouts  0.7 us (1%)
    pallas_call x1, Pallas kernels, on_device(): pl.pallas_call(functools.partial(kernel, rows_n, float(width * rows_n), c...  48 us

profile of v4, /device:TPU:72, one launch (start us, length us, event | category | flops | bytes accessed | tf_op | source)
XLA Modules:
  0.0 48.7 jit_solution(1161293322129451283)
XLA Ops:
  0.0 48.0 %clip_attention.1 = bf16[192,640]{1,0:T(8,128)(2,1)S(1)} custom-call(bf16[192,640]{1,0:T(8,128)(2,1)} %q_hbm.1, bf16[192,640]{1,0:T(8,128)(2,1)} %k_hbm.1, bf16[192,640]{1,0:T(8,128)(2,1)} %v.1, f32[640]{0:T(1024)} %gq_hbm.1, f32[640]{0:T(1024)} %gk_hbm.1, s32[1,192]{1,0:T(1,128)} %bitcast.2, f32[1,128]{1,0:T(1,128)} %constant.2.clone.freq_hbm, s32[2,4]{1,0:T(2,128)} %bitcast.3), custom_call_target="tpu_custom_call" | custom-call | tf_op jit(solution)/shard_map/clip_attention/pallas_call | solution.py:361
  48.0 0.7 %copy.10 = bf16[192,640]{1,0:T(8,128)(2,1)} copy(bf16[192,640]{1,0:T(8,128)(2,1)S(1)} %clip_attention.1) | data formatting | bytes 491520

commit v5 on v4

--- a/solution.py
+++ b/solution.py
@@ -91,7 +91,7 @@
             send(src.at[:, cols(zs[d])], dst, 2 + n, sem_zr.at[n, d], {"ctx": zpeer[d]})
 
     def four_to_z(n, src, dst):
-        for d in (1, 3, 2):
+        for d in (2, 1, 3) if n else (1, 3, 2):
             send(src.at[:, cols(4)], left(dst, z), 2 + n, sem_r.at[n], {"ctx": zpeer[d]})
 
     def to_near(n, src, dst, a):

time: 48.8 us -> 48.3 us (0.990)
  the two profiles are of different devices: /device:TPU:72 before, /device:TPU:80 now
where the time goes in v5:
time: 48.3 us; the launch traced here: 48.2 us
  Pallas kernels  47.4 us (98%)
  local copies, waits for them, and re-layouts  0.7 us (1%)
    pallas_call x1, Pallas kernels, on_device(): pl.pallas_call(functools.partial(kernel, rows_n, float(width * rows_n), c...  47.4 us

profile of v5, /device:TPU:80, one launch (start us, length us, event | category | flops | bytes accessed | tf_op | source)
XLA Modules:
  0.0 48.2 jit_solution(145015788945042149)
XLA Ops:
  0.0 47.4 %clip_attention.1 = bf16[192,640]{1,0:T(8,128)(2,1)S(1)} custom-call(bf16[192,640]{1,0:T(8,128)(2,1)} %q_hbm.1, bf16[192,640]{1,0:T(8,128)(2,1)} %k_hbm.1, bf16[192,640]{1,0:T(8,128)(2,1)} %v.1, f32[640]{0:T(1024)} %gq_hbm.1, f32[640]{0:T(1024)} %gk_hbm.1, s32[1,192]{1,0:T(1,128)} %bitcast.2, f32[1,128]{1,0:T(1,128)} %constant.2.clone.freq_hbm, s32[2,4]{1,0:T(2,128)} %bitcast.3), custom_call_target="tpu_custom_call" | custom-call | tf_op jit(solution)/shard_map/clip_attention/pallas_call | solution.py:361
  47.5 0.7 %copy.10 = bf16[192,640]{1,0:T(8,128)(2,1)} copy(bf16[192,640]{1,0:T(8,128)(2,1)S(1)} %clip_attention.1) | data formatting | bytes 491520
